TPU v7x, 128 devices: a whole 4x4x4 slice. The times are simulated.
128 devices in a mesh: pairs: 16 (over z, x), days: 8 (over y, core).
Axes of the slice: x: 4, y: 4, z: 4, core: 2. Of those that a mesh axis runs over, the one named last changes fastest.
Arguments:
- spectra: bfloat16 [8, 512, 2048], P('days', None, 'pairs'), may hold values from -6 to 6
- observed: bfloat16 [32, 64, 64, 128], P('pairs'), may hold values from -6 to 6
- pair_blocks: int32 [32, 2], replicated, may hold values from 0 to 7, as said below
- members: int32 [512], replicated, may hold values from 0 to 511, each once
- day_mask: int32 [32, 8], P('pairs'), may hold values from 0 to 1, as said below
Outputs:
- adjoint_spectra: float32 [8, 512, 2048], P('days', None, 'pairs')
Inputs may be any that keep to these rules, and one draw needn't show every extreme that they name: `pair_blocks`: each row holds two station block numbers, the first not above the second; no two rows are alike. `members`: every station appears once. `day_mask`: every listed pair is used on at least one day.
All inputs are finite; a program needn't handle non-finite values.
Results may differ from a plain program's by a relative error of at most 0.0025.
Values may be sent and summed in bfloat16 or wider, within the bound.
A program may use at most 64 MiB of HBM per device.

v0:
```python
import math

import jax
import jax.numpy as jnp
from jax import lax
from jax.sharding import PartitionSpec as P

B = 64
F = 1024
L = 128
SLOTS = 2
DAYS_DEV = 1
NBLK = 8


def dft_tables():
    column = jnp.arange(2 * F, dtype=jnp.int32)
    frequency = column // 128 * 64 + column % 64
    part_of = column % 128 // 64
    lag_of = jnp.arange(L, dtype=jnp.int32) - L // 2
    phase_idx = frequency[:, None] * lag_of[None, :] % (2 * F)
    angles = jnp.float32(math.pi) * phase_idx.astype(jnp.float32) / F
    norm_scale = 1.0 / math.sqrt(F)
    cosine = jnp.cos(angles) * norm_scale
    sine_part = jnp.sin(angles) * norm_scale
    forward = jnp.where(part_of[:, None] == 0, cosine, -sine_part).astype(jnp.bfloat16)
    backward = jnp.where(part_of[:, None] == 0, cosine, sine_part).T.astype(jnp.bfloat16)
    return (forward, backward)


def hilbert_table():
    lag_rows = jnp.arange(L, dtype=jnp.int32)[:, None]
    lag_cols = jnp.arange(L, dtype=jnp.int32)[None, :]
    offset = (lag_cols - lag_rows) % L
    is_odd = offset % 2 == 1
    angles = jnp.float32(math.pi) * offset.astype(jnp.float32) / L
    safe_sin = jnp.where(is_odd, jnp.sin(angles), jnp.float32(1.0))
    return jnp.where(is_odd, 2.0 / L * jnp.cos(angles) / safe_sin, jnp.float32(0.0))


def weighted_residual(stacked, observed_f, hilbert):
    flat_s = stacked.reshape(-1, L)
    flat_o = observed_f.reshape(-1, L)
    hil_s = jnp.dot(
        flat_s, hilbert, precision=lax.Precision.HIGHEST, preferred_element_type=jnp.float32
    )
    hil_o = jnp.dot(
        flat_o, hilbert, precision=lax.Precision.HIGHEST, preferred_element_type=jnp.float32
    )
    env_s = jnp.sqrt(flat_s * flat_s + hil_s * hil_s)
    env_o = jnp.sqrt(flat_o * flat_o + hil_o * hil_o)
    weight = (1.0 + env_s) / (1.0 + env_s + env_o)
    return ((flat_s - flat_o) * weight).reshape(stacked.shape)


def tile_parts(spec_block, tile_idx):
    tile_piece = lax.dynamic_slice_in_dim(spec_block, tile_idx * 128, 128, 3).astype(jnp.float32)
    return (tile_piece[..., :64], tile_piece[..., 64:])


def body(spectra, observed, pair_blocks, members, day_mask):
    my_pair = lax.axis_index("pairs")
    my_day = lax.axis_index("days")
    stations = spectra.shape[1]
    n_tiles = 2 * F // 128
    forward, backward = dft_tables()
    backward_f = backward.astype(jnp.float32)
    hilbert = hilbert_table()
    offsets = jnp.arange(B, dtype=jnp.int32)
    my_blocks = lax.dynamic_slice_in_dim(pair_blocks, my_pair * SLOTS, SLOTS, 0)
    mask_here = lax.dynamic_slice_in_dim(day_mask, my_day * DAYS_DEV, DAYS_DEV, 1).astype(
        jnp.float32
    )
    day_count = jnp.sum(day_mask.astype(jnp.float32), axis=1)
    day_share = mask_here / day_count[:, None]
    gathered = lax.all_gather(spectra, "pairs", axis=2, tiled=True)
    my_rows = members[my_blocks[:, :, None] * B + offsets[None, None, :]].reshape(-1)
    arrived = jnp.take(gathered, my_rows, axis=1)
    arrived = arrived.reshape(DAYS_DEV, SLOTS, 2, B, 2 * F)
    side_a = arrived[:, :, 0]
    side_b = arrived[:, :, 1]
    day_weight = mask_here.T[:, :, None, None]

    def forward_tile(tile_idx, accum):
        a_real, a_imag = tile_parts(side_a, tile_idx)
        b_real, b_imag = tile_parts(side_b, tile_idx)
        masked_real = a_real * day_weight
        masked_imag = a_imag * day_weight
        cross_real = jnp.einsum("dsaj,dsbj->sabdj", masked_real, b_real) + jnp.einsum(
            "dsaj,dsbj->sabdj", masked_imag, b_imag
        )
        cross_imag = jnp.einsum("dsaj,dsbj->sabdj", masked_imag, b_real) - jnp.einsum(
            "dsaj,dsbj->sabdj", masked_real, b_imag
        )
        cross_tile = jnp.concatenate([cross_real, cross_imag], axis=-1).astype(jnp.bfloat16)
        cross_tile = cross_tile.reshape(SLOTS * B * B, DAYS_DEV * 128)
        table_rows = jnp.tile(
            lax.dynamic_slice_in_dim(forward, tile_idx * 128, 128, 0), (DAYS_DEV, 1)
        )
        return accum + jnp.dot(cross_tile, table_rows, preferred_element_type=jnp.float32)

    partial_value = lax.fori_loop(
        0, n_tiles, forward_tile, jnp.zeros((SLOTS * B * B, L), jnp.float32)
    )
    partial_value = partial_value.reshape(SLOTS, B, B, L)
    summed = lax.psum(partial_value, "days")
    residual = weighted_residual(
        summed / day_count[:, None, None, None], observed.astype(jnp.float32), hilbert
    )
    residual_flat = residual.reshape(SLOTS * B * B, L)
    share_weight = day_share.T[:, :, None, None]

    def adjoint_tile(tile_idx, contrib):
        cols_here = lax.dynamic_slice_in_dim(backward_f, tile_idx * 128, 128, 1)
        response = jnp.dot(
            residual_flat,
            cols_here,
            precision=lax.Precision.HIGHEST,
            preferred_element_type=jnp.float32,
        ).reshape(SLOTS, B, B, 128)
        g_cos = response[..., :64]
        g_sin = response[..., 64:]
        a_real, a_imag = tile_parts(side_a, tile_idx)
        b_real, b_imag = tile_parts(side_b, tile_idx)
        adj_a_real = jnp.einsum("sabj,dsbj->dsaj", g_cos, b_real) + jnp.einsum(
            "sabj,dsbj->dsaj", g_sin, b_imag
        )
        adj_a_imag = jnp.einsum("sabj,dsbj->dsaj", g_cos, b_imag) - jnp.einsum(
            "sabj,dsbj->dsaj", g_sin, b_real
        )
        adj_b_real = jnp.einsum("sabj,dsaj->dsbj", g_cos, a_real) - jnp.einsum(
            "sabj,dsaj->dsbj", g_sin, a_imag
        )
        adj_b_imag = jnp.einsum("sabj,dsaj->dsbj", g_cos, a_imag) + jnp.einsum(
            "sabj,dsaj->dsbj", g_sin, a_real
        )
        new_a = jnp.concatenate([adj_a_real, adj_a_imag], axis=-1) * share_weight
        new_b = jnp.concatenate([adj_b_real, adj_b_imag], axis=-1) * share_weight
        both_sides = jnp.stack([new_a, new_b], axis=2)
        return lax.dynamic_update_slice_in_dim(contrib, both_sides, tile_idx * 128, 4)

    contrib = lax.fori_loop(
        0, n_tiles, adjoint_tile, jnp.zeros((DAYS_DEV, SLOTS, 2, B, 2 * F), jnp.float32)
    )
    contrib = contrib.reshape(DAYS_DEV, 2 * SLOTS, B, 2 * F)
    block_ids = jnp.arange(NBLK, dtype=jnp.int32)[:, None]
    onehot = (block_ids == my_blocks.reshape(-1)[None, :]).astype(jnp.float32)
    dense = jnp.einsum("nr,drbc->dnbc", onehot, contrib, precision=lax.Precision.HIGHEST)
    block_sum = lax.psum_scatter(dense, "pairs", scatter_dimension=3, tiled=True)
    flat_rows = block_sum.reshape(DAYS_DEV, NBLK * B, block_sum.shape[3])
    inverse = (
        jnp.zeros((stations,), jnp.int32).at[members].set(jnp.arange(stations, dtype=jnp.int32))
    )
    return jnp.take(flat_rows, inverse, axis=1)


def solution(mesh):
    return jax.shard_map(
        body,
        mesh=mesh,
        in_specs=(
            P("days", None, "pairs"),
            P("pairs", None, None, None),
            P(),
            P(),
            P("pairs", None),
        ),
        out_specs=P("days", None, "pairs"),
        check_vma=False,
    )
```

profile of v0, /device:TPU:1, one launch (start us, length us, event | category | flops | bytes accessed | tf_op | source)
XLA Modules:
  0.0 882.6 jit_solution(5188095857157093993)
XLA Ops:
  11.4 6.2 select_convert_fusion
  17.6 40.6 %all-gather.2.cloned.1.call-done = bf16[1,512,2048]{2,1,0:T(8,128)(2,1)} async-done(((bf16[1,512,128]{2,1,0:T(8,128)(2,1)}), bf16[1,512,2048]{2,1,0:T(8,128)(2,1)}) %all-gather.2.cloned.1.call-update) | async-done | bytes 2097168 | tf_op jit(solution)/shard_map/all_gather | solution.py:76
  67.4 254.9 %while.28 = (s32[]{:T(128)}, f32[8192,128]{1,0:T(8,128)}, bf16[1,2,64,2048]{2,1,3,0:T(2,128)(2,1)S(1)}, bf16[1,2,64,2048]{2,1,3,0:T(2,128)(2,1)S(1)}, f32[1,2,1,...) while((s32[]{:T(128)}, f32[8192,128]{1,0:T(8,128)}, ...), condition=%wide.region_2.3_spmd.clone, body=%wide.region_1.2_spmd.clone.sunk | while | flops 278970368 | bytes 25657664 | solution.py:102
  108.7 5.4 convolution_add_fusion.2
  124.7 5.4 convolution_add_fusion.2
  172.7 5.4 convolution_add_fusion.2
  188.8 5.4 convolution_add_fusion.2
  236.8 5.4 convolution_add_fusion.2
  252.8 5.4 convolution_add_fusion.2
  300.8 5.4 convolution_add_fusion.2
  316.8 5.4 convolution_add_fusion.2
  331.1 62.9 %all-reduce.2.cloned.1.call-done = f32[2,64,64,128]{3,2,1,0:T(8,128)} async-done(((f32[2,64,64,128]{3,2,1,0:T(8,128)}), f32[2,64,64,128]{3,2,1,0:T(8,128)}) %all-reduce.2.cloned.1.call-update) | async-done | bytes 4194320 | tf_op jit(solution)/shard_map/psum | solution.py:106
  401.7 5.6 fusion.24
  407.6 381.1 %while.27 = (s32[]{:T(128)}, f32[1,2,2,64,2048]{4,3,2,1,0:T(8,128)S(1)}, bf16[1,2,64,2048]{3,2,1,0:T(8,128)(2,1)}, f32[128,2048]{1,0:T(8,128)S(1)}, f32[8192,128...) while((s32[]{:T(128)}, ...), condition=%wide.region_6.7_spmd, body=%wide.region_5.6_spmd.sunk | while | flops 1619099648 | bytes 43516140 | solution.py:142
  407.8 8.1 convolution_bitcast_fusion.3
  415.9 5.6 copy.94
  422.4 6.8 multiply_reduce_fusion.10
  431.6 8.1 convolution_bitcast_fusion.3
  439.7 5.6 copy.94
  446.2 6.8 multiply_reduce_fusion.10
  455.5 8.1 convolution_bitcast_fusion.3
  463.6 5.6 copy.94
  470.1 6.8 multiply_reduce_fusion.10
  479.3 7.9 convolution_bitcast_fusion.3
  487.3 5.6 copy.94
  493.7 6.8 multiply_reduce_fusion.10
  503.0 8.1 convolution_bitcast_fusion.3
  511.1 5.6 copy.94
  517.6 6.8 multiply_reduce_fusion.10
  526.8 8.1 convolution_bitcast_fusion.3
  534.9 5.6 copy.94
  541.4 6.8 multiply_reduce_fusion.10
  550.6 8.1 convolution_bitcast_fusion.3
  558.8 5.6 copy.94
  565.3 6.8 multiply_reduce_fusion.10
  574.5 7.9 convolution_bitcast_fusion.3
  582.4 5.6 copy.94
  589.0 6.8 multiply_reduce_fusion.10
  598.2 8.1 convolution_bitcast_fusion.3
  606.3 5.6 copy.94
  612.8 6.8 multiply_reduce_fusion.10
  622.1 8.1 convolution_bitcast_fusion.3
  630.1 5.6 copy.94
  636.7 6.8 multiply_reduce_fusion.10
  646.0 8.1 convolution_bitcast_fusion.3
  654.1 5.6 copy.94
  660.6 6.8 multiply_reduce_fusion.10
  669.8 7.9 convolution_bitcast_fusion.3
  677.7 5.6 copy.94
  684.2 6.8 multiply_reduce_fusion.10
  693.5 8.1 convolution_bitcast_fusion.3
  701.6 5.6 copy.94
  708.1 6.8 multiply_reduce_fusion.10
  717.3 8.1 convolution_bitcast_fusion.3
  725.4 5.6 copy.94
  731.9 6.8 multiply_reduce_fusion.10
  741.1 8.1 convolution_bitcast_fusion.3
  749.2 5.6 copy.94
  755.8 6.8 multiply_reduce_fusion.10
  765.0 7.9 convolution_bitcast_fusion.3
  772.9 5.6 copy.94
  779.5 6.8 multiply_reduce_fusion.10
  788.7 5.8 convolution_bitcast_fusion.1
  797.0 76.2 %reduce-scatter.2.cloned.1.call-done = f32[1,8,64,128]{3,1,2,0:T(8,128)} async-done(((f32[1,8,64,2048]{3,1,2,0:T(8,128)}), f32[1,8,64,128]{3,1,2,0:T(8,128)}) %reduce-scatter.2.cloned.1.call-update) | async-done | bytes 262160 | tf_op jit(solution)/shard_map/reduce_scatter | solution.py:149
  (445 shorter events, 299.0 us)
Async XLA Ops:
  6.5 51.7 %all-gather.2.cloned.1.call-start = ((), (), s32[]{:S(2)}) async-start(), calls=%async_computation.1 | async-start | bytes 2228224 | tf_op jit(solution)/shard_map/all_gather | solution.py:76
  7.3 386.7 %all-reduce.2.cloned.1.call-start = ((), (), s32[]{:S(2)}) async-start(), calls=%async_computation.2 | async-start | bytes 8388608 | tf_op jit(solution)/shard_map/psum | solution.py:106
  78.0 4.1 copy-start.3
  78.0 4.1 copy-start.5
  82.1 1.3 copy-start.4
  92.7 5.4 copy-start.3
  92.7 5.4 copy-start.5
  98.1 1.3 copy-start.4
  108.7 5.4 copy-start.3
  108.7 5.4 copy-start.5
  114.1 1.3 copy-start.4
  124.7 5.4 copy-start.3
  124.7 5.4 copy-start.5
  130.1 1.3 copy-start.4
  140.7 5.4 copy-start.3
  140.7 5.4 copy-start.5
  146.1 1.3 copy-start.4
  156.7 5.4 copy-start.3
  156.7 5.4 copy-start.5
  162.1 1.3 copy-start.4
  172.7 5.4 copy-start.3
  172.7 5.4 copy-start.5
  178.2 1.3 copy-start.4
  188.8 5.4 copy-start.3
  188.8 5.4 copy-start.5
  194.2 1.3 copy-start.4
  204.8 5.4 copy-start.3
  204.8 5.4 copy-start.5
  210.2 1.3 copy-start.4
  220.8 5.4 copy-start.3
  220.8 5.4 copy-start.5
  226.2 1.3 copy-start.4
  236.8 5.4 copy-start.3
  236.8 5.4 copy-start.5
  242.2 1.3 copy-start.4
  252.8 5.4 copy-start.3
  252.8 5.4 copy-start.5
  268.8 5.4 copy-start.3
  268.8 5.4 copy-start.5
  284.8 5.4 copy-start.3
  284.8 5.4 copy-start.5
  300.8 5.4 copy-start.3
  300.8 5.4 copy-start.5
  316.8 5.4 copy-start.3
  316.8 5.4 copy-start.5
  322.3 550.9 %reduce-scatter.2.cloned.1.call-start = ((), (), s32[]{:S(2)}) async-start(), calls=%async_computation.3 | async-start | bytes 4456448 | tf_op jit(solution)/shard_map/reduce_scatter | solution.py:149
  396.7 5.0 copy-start.7
  422.4 6.9 copy-start
  446.2 6.9 copy-start
  470.1 6.9 copy-start
  493.7 6.9 copy-start
  517.6 6.9 copy-start
  541.4 6.9 copy-start
  565.3 6.9 copy-start
  589.0 6.9 copy-start
  612.8 6.9 copy-start
  636.7 6.9 copy-start
  660.6 6.9 copy-start
  684.2 6.9 copy-start
  708.1 6.9 copy-start
  731.9 6.9 copy-start
  755.8 6.9 copy-start
  779.5 6.9 copy-start
  788.7 5.8 copy-start.1
  (22 other events, 22.9 us)
Sparse Core Ops, SparseCore 0:
  9.4 48.7 all-gather.1
  322.4 71.5 all-reduce.1
  794.6 78.5 reduce-scatter.1
where the time goes:
time: 888 us; the launch traced here: 883 us
  other arithmetic  238 us (27%)
  matrix products  230 us (26%)
  local copies, waits for them, and re-layouts  218 us (25%)
  waiting for transfers between devices  180 us (20%)
  between operations  13.3 us (1%)
    dot_general x16, matrix products, adjoint_tile(): jnp.dot(residual_flat, cols_here, precision=lax.Precision.HIGHEST, prefer...  129 us
    dot_general x16, other arithmetic, adjoint_tile(): jnp.einsum('sabj,dsbj->dsaj', g_sin, b_imag)  109 us
    concatenate x32, local copies, waits for them, and re-layouts, forward_tile(): jnp.concatenate([cross_real, cross_imag], axis=-1).astype(jnp.bfloat16)  93 us
    dot_general x16, local copies, waits for them, and re-layouts, adjoint_tile(): jnp.dot(residual_flat, cols_here, precision=lax.Precision.HIGHEST, prefer...  89 us
    dot_general x16, matrix products, forward_tile(): jnp.dot(cross_tile, table_rows, preferred_element_type=jnp.float32)  85 us
    reduce_scatter x1, waiting for transfers between devices, body(): lax.psum_scatter(dense, 'pairs', scatter_dimension=3, tiled=True)  76.2 us
    psum x1, waiting for transfers between devices, body(): summed = lax.psum(partial_value, 'days')  62.9 us
    add x16, other arithmetic, forward_tile(): jnp.einsum('dsaj,dsbj->sabdj', masked_real, b_real)  55.8 us
  transfers between devices with their start and end apart: 3, of which 3 were waited for; matrix products, arithmetic and copies ran while one was open for 2% of the time, Pallas kernels for 0%

commit v1 on v0

v1 whole, which is shorter than its diff:
```python
import functools

import jax
import jax.numpy as jnp
import numpy as np
from jax import lax
from jax.experimental import pallas as pl
from jax.experimental.pallas import tpu as pltpu
from jax.sharding import PartitionSpec as P

B = 64
F = 1024
L = 128
NBLK = 8
NSTA = 512
N1 = 16
N2 = 8
NQ = 16
NY = 4
NC = NQ * NY
ROWS = 96
MESH = pl.DeviceIdType.MESH
F32 = jnp.float32
BF16 = jnp.bfloat16


def phase_tables():
    freq = 64 * np.arange(NQ)[:, None] + np.arange(128)[None, :] % 64
    sign = np.where(np.arange(128) < 64, -1.0, 1.0)[None, None, :]
    shift_a = N2 * np.arange(N1) - L // 2
    shift_b = -np.arange(N2)
    tables = []
    for shift in (shift_a, shift_b):
        turns = (freq[:, None, :] * shift[None, :, None]) % (2 * F)
        angle = np.pi * turns / F
        tables.append(np.cos(angle).astype(np.float32))
        tables.append((np.sin(angle) * sign).astype(np.float32))
    return tables


def hilbert_blocks():
    blocks = []
    for k in (1, 3, 5, 7):
        offset = (8 * (np.arange(N1)[:, None] - np.arange(N1)[None, :]) + k) % L
        angle = np.pi * offset / L
        value = 2.0 / L * np.cos(angle) / np.sin(angle)
        blocks.append(np.kron(value, np.eye(16)))
    exact = np.stack(blocks).astype(np.float32)
    high = exact.astype(jnp.bfloat16)
    low = (exact - high.astype(np.float32)).astype(jnp.bfloat16)
    return high, low


def dot(a, b):
    return lax.dot_general(a, b, (((1,), (0,)), ((), ())), preferred_element_type=F32)


def kernel(
    mask_ref, idc_ref, ids_ref, spec_ref, obs_ref, ca_ref, sa_ref, cb_ref, sb_ref,
    kh_ref, kl_ref, out_ref,
    stage, xin, amod, bmod, acc, acc_in, envo, rfull, rturn, tbuf, ubuf, outb, rin,
    send_a, recv_a, send_d, recv_d, send_x, recv_x,
):
    q_me = lax.axis_index("pairs")
    d_me = lax.axis_index("days")
    y_me = d_me // 2
    k_me = lax.rem(d_me, 2)
    c_me = q_me * NY + y_me
    z_me = q_me // 4
    x_me = lax.rem(q_me, 4)
    pp = y_me // 2
    partner = (q_me, y_me * 2 + 1 - k_me)

    barrier = pltpu.get_barrier_semaphore()

    def greet(c, carry):
        @pl.when(c != c_me)
        def _():
            pl.semaphore_signal(
                barrier, inc=1, device_id=(c // NY, lax.rem(c, NY) * 2 + k_me), device_id_type=MESH
            )

        return carry

    lax.fori_loop(0, NC, greet, 0)
    pl.semaphore_signal(barrier, inc=1, device_id=partner, device_id_type=MESH)

    pl.semaphore_wait(barrier, NC)

    def target(step):
        q = lax.rem(z_me + step // 4, 4) * 4 + lax.rem(x_me + lax.rem(step, 4), 4)
        return q

    def source(step):
        q = lax.rem(z_me + 4 - step // 4, 4) * 4 + lax.rem(x_me + 4 - lax.rem(step, 4), 4)
        return q

    def copy_a(c, slot):
        return pltpu.make_async_remote_copy(
            src_ref=stage.at[c],
            dst_ref=xin.at[slot],
            send_sem=send_a.at[c],
            recv_sem=recv_a.at[slot],
            device_id=(c // NY, lax.rem(c, NY) * 2 + k_me),
            device_id_type=MESH,
        )

    def copy_d(c, slot):
        return pltpu.make_async_remote_copy(
            src_ref=outb.at[c],
            dst_ref=rin.at[slot],
            send_sem=send_d.at[c],
            recv_sem=recv_d.at[slot],
            device_id=(c // NY, lax.rem(c, NY) * 2 + k_me),
            device_id_type=MESH,
        )

    lane_q = lax.broadcasted_iota(jnp.int32, (NY * ROWS, NQ), 1)
    lane_s = lax.broadcasted_iota(jnp.int32, (NY * ROWS, NSTA), 1)

    def send_all(step, carry):
        q = target(step)
        row_id = jnp.sum(jnp.where(lane_q == q, idc_ref[...], 0), axis=1, keepdims=True)
        select = (lane_s == row_id).astype(F32).astype(BF16)
        rows = dot(select, spec_ref[...]).astype(BF16)
        stage[pl.ds(q * NY, NY)] = rows.reshape(NY, ROWS, 128)
        for i in range(NY):
            c = q * NY + lax.rem(y_me + i, NY)

            @pl.when(c != c_me)
            def _():
                copy_a(c, c_me).start()

        return carry

    lax.fori_loop(0, NQ, send_all, 0)
    xin[c_me] = stage[c_me]

    count = jnp.zeros((1, 128), F32)
    for d in range(8):
        count = count + mask_ref[pp, d].astype(F32)

    def hilbert(high, low):
        lane = lax.broadcasted_iota(jnp.int32, (256, 512), 1)
        total = None
        for j, k in enumerate((1, 3, 5, 7)):
            part = dot(kh_ref[j], high) + dot(kl_ref[j], high)
            if low is not None:
                part = part + dot(kh_ref[j], low)
            part = pltpu.roll(part, 64 * k, 1)
            part = jnp.where(lane < 64 * k, pltpu.roll(part, 16, 0), part)
            total = part if total is None else total + part
        return total

    obs_f = obs_ref[...].astype(F32)
    hil_o = hilbert(obs_ref[...], None)
    envo[...] = jnp.sqrt(obs_f * obs_f + hil_o * hil_o)

    acc[...] = jnp.zeros_like(acc)

    def forward(step, carry):
        q = source(step)
        for y in range(NY):
            c = q * NY + y

            @pl.when(c != c_me)
            def _():
                copy_a(c, c).wait_recv()

        for y in range(NY):
            keep = mask_ref[pp, 2 * y + k_me].astype(F32)
            x = xin[q * NY + y].astype(F32) * keep
            xr = pltpu.roll(x, 64, 1)
            lanes = slice(y * 128, (y + 1) * 128)
            for h in range(2):
                rows = slice(h * 16, (h + 1) * 16)
                for n in range(N1):
                    turned = x[rows] * ca_ref[q, n : n + 1, :] + xr[rows] * sa_ref[q, n : n + 1, :]
                    amod[q, h * 256 + n * 16 : h * 256 + (n + 1) * 16, lanes] = turned.astype(BF16)
            for n in range(N2):
                turned = x[32:] * cb_ref[q, n : n + 1, :] + xr[32:] * sb_ref[q, n : n + 1, :]
                bmod[q, n * 64 : (n + 1) * 64, lanes] = turned.astype(BF16)
        for h in range(2):
            acc[h] += lax.dot_general(
                amod[q, h * 256 : (h + 1) * 256, :],
                bmod[q],
                (((1,), (1,)), ((), ())),
                preferred_element_type=F32,
            )
        return carry

    lax.fori_loop(0, NQ, forward, 0)

    swap = pltpu.make_async_remote_copy(
        src_ref=acc.at[1 - k_me],
        dst_ref=acc_in,
        send_sem=send_x.at[0],
        recv_sem=recv_x.at[0],
        device_id=partner,
        device_id_type=MESH,
    )
    swap.start()
    swap.wait_recv()
    lanes_count = jnp.concatenate([count] * 4, axis=1)
    stacked = (acc[k_me] + acc_in[...]) * (1.0 / 32.0) / lanes_count
    high = stacked.astype(BF16)
    low = (stacked - high.astype(F32)).astype(BF16)
    hil_s = hilbert(high, low)
    env_s = jnp.sqrt(stacked * stacked + hil_s * hil_s)
    residual = (stacked - obs_ref[...].astype(F32)) * (
        (1.0 + env_s) / (1.0 + env_s + envo[...])
    )
    rfull[k_me] = (residual * (1.0 / 32.0) / lanes_count).astype(BF16)
    share = pltpu.make_async_remote_copy(
        src_ref=rfull.at[k_me],
        dst_ref=rfull.at[k_me],
        send_sem=send_x.at[1],
        recv_sem=recv_x.at[1],
        device_id=partner,
        device_id_type=MESH,
    )
    share.start()
    pltpu.make_async_remote_copy(
        src_ref=rfull.at[1 - k_me],
        dst_ref=rfull.at[1 - k_me],
        send_sem=send_x.at[1],
        recv_sem=recv_x.at[1],
        device_id=partner,
        device_id_type=MESH,
    ).wait_recv()
    rturn[...] = rfull[...].reshape(512, 512).T

    def adjoint(step, carry):
        q = target(step)
        for h in range(2):
            tbuf[h * 256 : (h + 1) * 256, :] = dot(rfull[h], bmod[q])
        for h in range(2):
            ubuf[h * 256 : (h + 1) * 256, :] = dot(rturn[h * 256 : (h + 1) * 256, :], amod[q])
        for y in range(NY):
            c = q * NY + y
            lanes = slice(y * 128, (y + 1) * 128)
            for h in range(2):
                straight = jnp.zeros((16, 128), F32)
                crossed = jnp.zeros((16, 128), F32)
                for n in range(N1):
                    t = tbuf[h * 256 + n * 16 : h * 256 + (n + 1) * 16, lanes]
                    straight = straight + t * ca_ref[q, n : n + 1, :]
                    crossed = crossed + t * sa_ref[q, n : n + 1, :]
                outb[c, h * 16 : (h + 1) * 16, :] = (
                    straight + pltpu.roll(crossed, 64, 1)
                ).astype(BF16)
            straight = jnp.zeros((64, 128), F32)
            crossed = jnp.zeros((64, 128), F32)
            for n in range(N2):
                u = ubuf[n * 64 : (n + 1) * 64, lanes]
                straight = straight + u * cb_ref[q, n : n + 1, :]
                crossed = crossed + u * sb_ref[q, n : n + 1, :]
            outb[c, 32:96, :] = (straight + pltpu.roll(crossed, 64, 1)).astype(BF16)
        for y in range(NY):
            c = q * NY + y

            @pl.when(c != c_me)
            def _():
                copy_d(c, c_me).start()

            @pl.when(c == c_me)
            def _():
                rin[c_me] = outb[c_me]

        return carry

    lax.fori_loop(0, NQ, adjoint, 0)

    out_ref[...] = jnp.zeros_like(out_ref)
    station = lax.broadcasted_iota(jnp.int32, (NSTA, NY * ROWS), 0)

    def gather(step, carry):
        q = source(step)
        for y in range(NY):
            c = q * NY + y

            @pl.when(c != c_me)
            def _():
                copy_d(c, c).wait_recv()

        place = (station == ids_ref[q]).astype(F32).astype(BF16)
        out_ref[...] += dot(place, rin[pl.ds(q * NY, NY)].reshape(NY * ROWS, 128))
        return carry

    lax.fori_loop(0, NQ, gather, 0)

    def drain(c, carry):
        @pl.when(c != c_me)
        def _():
            copy_a(c, c_me).wait_send()
            copy_d(c, c_me).wait_send()

        return carry

    lax.fori_loop(0, NC, drain, 0)
    swap.wait_send()
    share.wait_send()


def body(spectra, observed, pair_blocks, members, day_mask):
    y_me = lax.axis_index("days") // 2
    k_me = lax.rem(lax.axis_index("days"), 2)
    blocks = members.reshape(NBLK, B).astype(F32)
    pick = (pair_blocks[:, :, None] == jnp.arange(NBLK)[None, None, :]).astype(F32)
    ids = jnp.einsum("psn,nr->psr", pick, blocks, precision=lax.Precision.HIGHEST)
    ids = ids.astype(jnp.int32)
    ids_a = ids[:, 0].reshape(NQ, NY, 32)
    ids_b = jnp.broadcast_to(ids[:, 1].reshape(NQ, 2, 1, B), (NQ, 2, 2, B)).reshape(NQ, NY, B)
    ids_all = jnp.concatenate([ids_a, ids_b], axis=2).reshape(NQ, NY * ROWS)
    obs = lax.dynamic_slice(
        observed,
        (y_me // 2, lax.rem(y_me, 2) * 32 + k_me * 16, 0, 0),
        (1, 16, B, L),
    )
    obs = obs.reshape(16, B, N1, N2).transpose(2, 0, 3, 1).reshape(256, 512)
    ca, sa, cb, sb = phase_tables()
    kh, kl = hilbert_blocks()
    vm = pl.BlockSpec(memory_space=pltpu.VMEM)
    sm = pl.BlockSpec(memory_space=pltpu.SMEM)
    return pl.pallas_call(
        kernel,
        out_shape=jax.ShapeDtypeStruct((NSTA, 128), F32),
        in_specs=[sm] + [vm] * 10,
        out_specs=vm,
        scratch_shapes=[
            pltpu.VMEM((NC, ROWS, 128), BF16),
            pltpu.VMEM((NC, ROWS, 128), BF16),
            pltpu.VMEM((NQ, 512, 512), BF16),
            pltpu.VMEM((NQ, 512, 512), BF16),
            pltpu.VMEM((2, 256, 512), F32),
            pltpu.VMEM((256, 512), F32),
            pltpu.VMEM((256, 512), F32),
            pltpu.VMEM((2, 256, 512), BF16),
            pltpu.VMEM((512, 512), BF16),
            pltpu.VMEM((512, 512), F32),
            pltpu.VMEM((512, 512), F32),
            pltpu.VMEM((NC, ROWS, 128), BF16),
            pltpu.VMEM((NC, ROWS, 128), BF16),
            pltpu.SemaphoreType.DMA((NC,)),
            pltpu.SemaphoreType.DMA((NC,)),
            pltpu.SemaphoreType.DMA((NC,)),
            pltpu.SemaphoreType.DMA((NC,)),
            pltpu.SemaphoreType.DMA((2,)),
            pltpu.SemaphoreType.DMA((2,)),
        ],
        compiler_params=pltpu.CompilerParams(
            collective_id=0, has_side_effects=True, vmem_limit_bytes=60 * 1024 * 1024
        ),
        name="stack_adjoint",
    )(
        day_mask,
        ids_all.T,
        ids_all.reshape(NQ, 1, NY * ROWS),
        spectra[0],
        obs,
        ca,
        sa,
        cb,
        sb,
        kh,
        kl,
    )[None]


def solution(mesh):
    return jax.shard_map(
        body,
        mesh=mesh,
        in_specs=(
            P("days", None, "pairs"),
            P("pairs", None, None, None),
            P(),
            P(),
            P("pairs", None),
        ),
        out_specs=P("days", None, "pairs"),
        check_vma=False,
    )
```

time: 888 us -> 84.8 us (0.10)
  the two profiles are of different devices: /device:TPU:1 before, /device:TPU:50 now
where the time goes in v1:
time: 84.8 us; the launch traced here: 84.6 us
  Pallas kernels  77.9 us (92%)
  local copies, waits for them, and re-layouts  6.36 us (8%)
    pallas_call x1, Pallas kernels, body(): pl.pallas_call(kernel, out_shape=jax.ShapeDtypeStruct((NSTA, 128), F32),...  77.9 us
    unnamed x8, local copies, waits for them, and re-layouts  3.5 us

profile of v1, /device:TPU:50, one launch (start us, length us, event | category | flops | bytes accessed | tf_op | source)
XLA Modules:
  0.0 84.6 jit_solution(17114701644267769907)
XLA Ops:
  0.0 0.0 copy-start
  0.0 0.0 copy-start.1
  0.0 0.0 copy-start.2
  0.1 1.5 %copy-done = bf16[2,64,64,128]{3,2,1,0:T(8,128)(2,1)S(1)} copy-done((bf16[2,64,64,128]{3,2,1,0:T(8,128)(2,1)S(1)}, bf16[2,64,64,128]{3,2,1,0:T(8,128)(2,1)}, u32[]{:S(2)}) %copy-start) | copy-done | bytes 2097176
  1.6 0.3 copy.16
  1.9 0.1 copy.15
  2.0 1.0 %reshape.19.obs_ref = bf16[256,512]{1,0:T(8,128)(2,1)} reshape(bf16[16,16,8,64]{3,2,1,0:T(8,128)(2,1)S(1)} %copy.15) | data formatting | bytes 524288 | tf_op jit(solution)/shard_map/reshape | solution.py:320
  3.1 0.0 copy-done.1
  3.1 0.1 reshape.20
  3.2 0.0 copy-done.2
  3.2 0.2 convolution_convert_fusion
  3.4 0.1 reshape_squeeze.4
  3.5 0.1 pad_add_fusion
  3.6 0.8 copy.13
  4.4 0.7 reshape_reshape.3.ids_ref
  5.1 77.9 %stack_adjoint.1 = f32[512,128]{1,0:T(8,128)} custom-call(s32[2,8]{1,0:T(2,128)} %mask_ref.1, s32[384,16]{1,0:T(8,128)} %bitcast.17, s32[16,1,384]{2,1,0:T(1,128)} %reshape_reshape.3.ids_ref, bf16[512,128]{1,0:T(8,128)(2,1)} %bitcast.18, bf16[256,512]{1,0:T(8,128)(2,1)} %reshape.19.obs_ref, f32[16,16,128]{2,1,0:T(8,128)} %constant.45.clone.ca_ref, ...), custom_call_target="tpu_custom_call" | custom-call | tf_op jit(solution)/shard_map/stack_adjoint/pallas_call | solution.py:325
  83.0 1.7 %copy.18 = f32[1,512,128]{2,1,0:T(8,128)} copy(f32[1,512,128]{2,1,0:T(8,128)} %bitcast.16) | data formatting | bytes 524288
  (4 shorter events, 0.0 us)
Async XLA Ops:
  0.0 1.6 %copy-start = (bf16[2,64,64,128]{3,2,1,0:T(8,128)(2,1)S(1)}, bf16[2,64,64,128]{3,2,1,0:T(8,128)(2,1)}, u32[]{:S(2)}) copy-start(bf16[2,64,64,128]{3,2,1,0:T(8,128)(2,1)} %param.12) | copy-start | bytes 6291460
  0.0 3.1 %copy-start.1 = (s32[512]{0:T(512)S(1)}, s32[512]{0:T(512)}, u32[]{:S(2)}) copy-start(s32[512]{0:T(512)} %param.14) | copy-start | bytes 6148
  0.0 3.1 %copy-start.2 = (s32[32,2]{0,1:T(2,128)S(1)}, s32[32,2]{0,1:T(2,128)}, u32[]{:S(2)}) copy-start(s32[32,2]{0,1:T(2,128)} %param.13) | copy-start | bytes 772

commit v2 on v1

--- a/solution.py
+++ b/solution.py
@@ -27,28 +27,25 @@
 def phase_tables():
     freq = 64 * np.arange(NQ)[:, None] + np.arange(128)[None, :] % 64
     sign = np.where(np.arange(128) < 64, -1.0, 1.0)[None, None, :]
-    shift_a = N2 * np.arange(N1) - L // 2
-    shift_b = -np.arange(N2)
     tables = []
-    for shift in (shift_a, shift_b):
+    for shift in (N2 * np.arange(N1) - L // 2, -np.arange(N2)):
         turns = (freq[:, None, :] * shift[None, :, None]) % (2 * F)
         angle = np.pi * turns / F
-        tables.append(np.cos(angle).astype(np.float32))
-        tables.append((np.sin(angle) * sign).astype(np.float32))
-    return tables
-
-
-def hilbert_blocks():
+        tables += [np.cos(angle), np.sin(angle) * sign]
+    return np.concatenate(tables, axis=1).astype(np.float32)
+
+
+CA, SA, CB, SB = 0, N1, 2 * N1, 2 * N1 + N2
+
+
+def hilbert_band():
     blocks = []
-    for k in (1, 3, 5, 7):
+    for k in range(7, -7, -2):
         offset = (8 * (np.arange(N1)[:, None] - np.arange(N1)[None, :]) + k) % L
         angle = np.pi * offset / L
         value = 2.0 / L * np.cos(angle) / np.sin(angle)
         blocks.append(np.kron(value, np.eye(16)))
-    exact = np.stack(blocks).astype(np.float32)
-    high = exact.astype(jnp.bfloat16)
-    low = (exact - high.astype(np.float32)).astype(jnp.bfloat16)
-    return high, low
+    return np.concatenate(blocks, axis=1).astype(np.float32).astype(jnp.bfloat16)
 
 
 def dot(a, b):
@@ -56,10 +53,10 @@
 
 
 def kernel(
-    mask_ref, idc_ref, ids_ref, spec_ref, obs_ref, ca_ref, sa_ref, cb_ref, sb_ref,
-    kh_ref, kl_ref, out_ref,
-    stage, xin, amod, bmod, acc, acc_in, envo, rfull, rturn, tbuf, ubuf, outb, rin,
-    send_a, recv_a, send_d, recv_d, send_x, recv_x,
+    mask_ref, ids_ref, spec_ref, obs_hbm, tab_hbm, band_hbm, out_ref,
+    stage, xin, amod, bmod, acc, acc_in, obsr, obst, obsf, envo, xst, idc, tab, band,
+    rfull, rturn, tbuf, ubuf, outb, rin,
+    send_a, recv_a, send_d, recv_d, send_x, recv_x, load,
 ):
     q_me = lax.axis_index("pairs")
     d_me = lax.axis_index("days")
@@ -73,6 +70,15 @@
 
     barrier = pltpu.get_barrier_semaphore()
 
+    row_a = lax.rem(y_me, 2) * 32 + k_me * 16
+    loads = [
+        pltpu.make_async_copy(obs_hbm.at[pp, pl.ds(row_a, 16)], obsr, load.at[0]),
+        pltpu.make_async_copy(band_hbm, band, load.at[1]),
+        pltpu.make_async_copy(tab_hbm, tab, load.at[2]),
+    ]
+    for copy in loads:
+        copy.start()
+
     def greet(c, carry):
         @pl.when(c != c_me)
         def _():
@@ -85,15 +91,32 @@
     lax.fori_loop(0, NC, greet, 0)
     pl.semaphore_signal(barrier, inc=1, device_id=partner, device_id_type=MESH)
 
+    idc[...] = ids_ref[...].astype(F32).T
+    lane_q = lax.broadcasted_iota(jnp.int32, (NY * ROWS, NQ), 1)
+    lane_s = lax.broadcasted_iota(jnp.int32, (NY * ROWS, NSTA), 1).astype(F32)
+
+    def fill(q, carry):
+        row_id = jnp.sum(jnp.where(lane_q == q, idc[...], 0.0), axis=1, keepdims=True)
+        select = (lane_s == row_id).astype(F32).astype(BF16)
+        rows = dot(select, spec_ref[...]).astype(BF16)
+        stage[pl.ds(q * NY, NY)] = rows.reshape(NY, ROWS, 128)
+        return carry
+
+    lax.fori_loop(0, NQ, fill, 0)
     pl.semaphore_wait(barrier, NC)
 
+    def offsets(step):
+        dx = lax.rem(17 - step, 4)
+        dz = lax.rem((15 - step) // 4 + 2 + dx, 4)
+        return dx, dz
+
     def target(step):
-        q = lax.rem(z_me + step // 4, 4) * 4 + lax.rem(x_me + lax.rem(step, 4), 4)
-        return q
+        dx, dz = offsets(step)
+        return lax.rem(z_me + dz, 4) * 4 + lax.rem(x_me + dx, 4)
 
     def source(step):
-        q = lax.rem(z_me + 4 - step // 4, 4) * 4 + lax.rem(x_me + 4 - lax.rem(step, 4), 4)
-        return q
+        dx, dz = offsets(step)
+        return lax.rem(z_me + 4 - dz, 4) * 4 + lax.rem(x_me + 4 - dx, 4)
 
     def copy_a(c, slot):
         return pltpu.make_async_remote_copy(
@@ -115,17 +138,10 @@
             device_id_type=MESH,
         )
 
-    lane_q = lax.broadcasted_iota(jnp.int32, (NY * ROWS, NQ), 1)
-    lane_s = lax.broadcasted_iota(jnp.int32, (NY * ROWS, NSTA), 1)
-
     def send_all(step, carry):
         q = target(step)
-        row_id = jnp.sum(jnp.where(lane_q == q, idc_ref[...], 0), axis=1, keepdims=True)
-        select = (lane_s == row_id).astype(F32).astype(BF16)
-        rows = dot(select, spec_ref[...]).astype(BF16)
-        stage[pl.ds(q * NY, NY)] = rows.reshape(NY, ROWS, 128)
-        for i in range(NY):
-            c = q * NY + lax.rem(y_me + i, NY)
+        for dy in (2, 1, 3, 0):
+            c = q * NY + lax.rem(y_me + dy, NY)
 
             @pl.when(c != c_me)
             def _():
@@ -140,23 +156,44 @@
     for d in range(8):
         count = count + mask_ref[pp, d].astype(F32)
 
-    def hilbert(high, low):
-        lane = lax.broadcasted_iota(jnp.int32, (256, 512), 1)
-        total = None
-        for j, k in enumerate((1, 3, 5, 7)):
-            part = dot(kh_ref[j], high) + dot(kl_ref[j], high)
-            if low is not None:
-                part = part + dot(kh_ref[j], low)
-            part = pltpu.roll(part, 64 * k, 1)
-            part = jnp.where(lane < 64 * k, pltpu.roll(part, 16, 0), part)
-            total = part if total is None else total + part
-        return total
-
-    obs_f = obs_ref[...].astype(F32)
-    hil_o = hilbert(obs_ref[...], None)
+    lane = lax.broadcasted_iota(jnp.int32, (1, 128), 1)
+
+    def hilbert(value):
+        for j in range(4):
+            swapped = pltpu.roll(value[:, j * 128 : (j + 1) * 128], 64, 1)
+            xst[j * 256 : (j + 1) * 256, :] = swapped.astype(BF16)
+        part = [dot(band[:, (3 - t) * 256 : (7 - t) * 256], xst[...]) for t in range(4)]
+        wrapped = [pltpu.roll(part[3], 16, 0)] + part
+        return jnp.concatenate(
+            [jnp.where(lane < 64, wrapped[j], wrapped[j + 1]) for j in range(4)], axis=1
+        )
+
+    loads[0].wait()
+
+    def turn(a, carry):
+        one = obsr[a].astype(F32)
+        obst[pl.ds(pl.multiple_of(a * 128, 128), 128), :] = jnp.concatenate([one, one], axis=0).T
+        return carry
+
+    lax.fori_loop(0, 16, turn, 0)
+
+    def place_lags(n, carry):
+        for j in range(4):
+            first = obst[pl.ds(n * 8 + 2 * j, 16, stride=128), :]
+            second = obst[pl.ds(n * 8 + 2 * j + 1, 16, stride=128), :]
+            obsf[pl.ds(pl.multiple_of(n * 16, 16), 16), j * 128 : (j + 1) * 128] = jnp.where(
+                lane < 64, first, second
+            )
+        return carry
+
+    lax.fori_loop(0, N1, place_lags, 0)
+    loads[1].wait()
+    obs_f = obsf[...]
+    hil_o = hilbert(obs_f)
     envo[...] = jnp.sqrt(obs_f * obs_f + hil_o * hil_o)
 
     acc[...] = jnp.zeros_like(acc)
+    loads[2].wait()
 
     def forward(step, carry):
         q = source(step)
@@ -175,10 +212,10 @@
             for h in range(2):
                 rows = slice(h * 16, (h + 1) * 16)
                 for n in range(N1):
-                    turned = x[rows] * ca_ref[q, n : n + 1, :] + xr[rows] * sa_ref[q, n : n + 1, :]
+                    turned = x[rows] * tab[q, CA + n : CA + n + 1, :] + xr[rows] * tab[q, SA + n : SA + n + 1, :]
                     amod[q, h * 256 + n * 16 : h * 256 + (n + 1) * 16, lanes] = turned.astype(BF16)
             for n in range(N2):
-                turned = x[32:] * cb_ref[q, n : n + 1, :] + xr[32:] * sb_ref[q, n : n + 1, :]
+                turned = x[32:] * tab[q, CB + n : CB + n + 1, :] + xr[32:] * tab[q, SB + n : SB + n + 1, :]
                 bmod[q, n * 64 : (n + 1) * 64, lanes] = turned.astype(BF16)
         for h in range(2):
             acc[h] += lax.dot_general(
@@ -203,11 +240,9 @@
     swap.wait_recv()
     lanes_count = jnp.concatenate([count] * 4, axis=1)
     stacked = (acc[k_me] + acc_in[...]) * (1.0 / 32.0) / lanes_count
-    high = stacked.astype(BF16)
-    low = (stacked - high.astype(F32)).astype(BF16)
-    hil_s = hilbert(high, low)
+    hil_s = hilbert(stacked)
     env_s = jnp.sqrt(stacked * stacked + hil_s * hil_s)
-    residual = (stacked - obs_ref[...].astype(F32)) * (
+    residual = (stacked - obsf[...]) * (
         (1.0 + env_s) / (1.0 + env_s + envo[...])
     )
     rfull[k_me] = (residual * (1.0 / 32.0) / lanes_count).astype(BF16)
@@ -244,8 +279,8 @@
                 crossed = jnp.zeros((16, 128), F32)
                 for n in range(N1):
                     t = tbuf[h * 256 + n * 16 : h * 256 + (n + 1) * 16, lanes]
-                    straight = straight + t * ca_ref[q, n : n + 1, :]
-                    crossed = crossed + t * sa_ref[q, n : n + 1, :]
+                    straight = straight + t * tab[q, CA + n : CA + n + 1, :]
+                    crossed = crossed + t * tab[q, SA + n : SA + n + 1, :]
                 outb[c, h * 16 : (h + 1) * 16, :] = (
                     straight + pltpu.roll(crossed, 64, 1)
                 ).astype(BF16)
@@ -253,8 +288,8 @@
             crossed = jnp.zeros((64, 128), F32)
             for n in range(N2):
                 u = ubuf[n * 64 : (n + 1) * 64, lanes]
-                straight = straight + u * cb_ref[q, n : n + 1, :]
-                crossed = crossed + u * sb_ref[q, n : n + 1, :]
+                straight = straight + u * tab[q, CB + n : CB + n + 1, :]
+                crossed = crossed + u * tab[q, SB + n : SB + n + 1, :]
             outb[c, 32:96, :] = (straight + pltpu.roll(crossed, 64, 1)).astype(BF16)
         for y in range(NY):
             c = q * NY + y
@@ -283,7 +318,7 @@
             def _():
                 copy_d(c, c).wait_recv()
 
-        place = (station == ids_ref[q]).astype(F32).astype(BF16)
+        place = (station == ids_ref[pl.ds(q, 1), :]).astype(F32).astype(BF16)
         out_ref[...] += dot(place, rin[pl.ds(q * NY, NY)].reshape(NY * ROWS, 128))
         return carry
 
@@ -303,8 +338,6 @@
 
 
 def body(spectra, observed, pair_blocks, members, day_mask):
-    y_me = lax.axis_index("days") // 2
-    k_me = lax.rem(lax.axis_index("days"), 2)
     blocks = members.reshape(NBLK, B).astype(F32)
     pick = (pair_blocks[:, :, None] == jnp.arange(NBLK)[None, None, :]).astype(F32)
     ids = jnp.einsum("psn,nr->psr", pick, blocks, precision=lax.Precision.HIGHEST)
@@ -312,20 +345,13 @@
     ids_a = ids[:, 0].reshape(NQ, NY, 32)
     ids_b = jnp.broadcast_to(ids[:, 1].reshape(NQ, 2, 1, B), (NQ, 2, 2, B)).reshape(NQ, NY, B)
     ids_all = jnp.concatenate([ids_a, ids_b], axis=2).reshape(NQ, NY * ROWS)
-    obs = lax.dynamic_slice(
-        observed,
-        (y_me // 2, lax.rem(y_me, 2) * 32 + k_me * 16, 0, 0),
-        (1, 16, B, L),
-    )
-    obs = obs.reshape(16, B, N1, N2).transpose(2, 0, 3, 1).reshape(256, 512)
-    ca, sa, cb, sb = phase_tables()
-    kh, kl = hilbert_blocks()
     vm = pl.BlockSpec(memory_space=pltpu.VMEM)
     sm = pl.BlockSpec(memory_space=pltpu.SMEM)
+    hbm = pl.BlockSpec(memory_space=pltpu.HBM)
     return pl.pallas_call(
         kernel,
         out_shape=jax.ShapeDtypeStruct((NSTA, 128), F32),
-        in_specs=[sm] + [vm] * 10,
+        in_specs=[sm, vm, vm, hbm, hbm, hbm],
         out_specs=vm,
         scratch_shapes=[
             pltpu.VMEM((NC, ROWS, 128), BF16),
@@ -334,7 +360,14 @@
             pltpu.VMEM((NQ, 512, 512), BF16),
             pltpu.VMEM((2, 256, 512), F32),
             pltpu.VMEM((256, 512), F32),
+            pltpu.VMEM((16, B, L), BF16),
+            pltpu.VMEM((16 * L, 128), F32),
             pltpu.VMEM((256, 512), F32),
+            pltpu.VMEM((256, 512), F32),
+            pltpu.VMEM((4 * 256, 128), BF16),
+            pltpu.VMEM((NY * ROWS, NQ), F32),
+            pltpu.VMEM((NQ, 2 * (N1 + N2), 128), F32),
+            pltpu.VMEM((256, 7 * 256), BF16),
             pltpu.VMEM((2, 256, 512), BF16),
             pltpu.VMEM((512, 512), BF16),
             pltpu.VMEM((512, 512), F32),
@@ -347,23 +380,19 @@
             pltpu.SemaphoreType.DMA((NC,)),
             pltpu.SemaphoreType.DMA((2,)),
             pltpu.SemaphoreType.DMA((2,)),
+            pltpu.SemaphoreType.DMA((3,)),
         ],
         compiler_params=pltpu.CompilerParams(
-            collective_id=0, has_side_effects=True, vmem_limit_bytes=60 * 1024 * 1024
+            collective_id=0, has_side_effects=True, vmem_limit_bytes=56000000
         ),
         name="stack_adjoint",
     )(
         day_mask,
-        ids_all.T,
-        ids_all.reshape(NQ, 1, NY * ROWS),
+        ids_all,
         spectra[0],
-        obs,
-        ca,
-        sa,
-        cb,
-        sb,
-        kh,
-        kl,
+        observed,
+        phase_tables(),
+        hilbert_band(),
     )[None]
 
 

time: 84.8 us -> 70.4 us (0.83)
  the two profiles are of different devices: /device:TPU:50 before, /device:TPU:1 now
where the time goes in v2:
time: 70.4 us; the launch traced here: 70.2 us
  Pallas kernels  66 us (94%)
  local copies, waits for them, and re-layouts  2.55 us (4%)
  matrix products  0.89 us (1%)
  other arithmetic  0.77 us (1%)
    pallas_call x1, Pallas kernels, body(): pl.pallas_call(kernel, out_shape=jax.ShapeDtypeStruct((NSTA, 128), F32),...  66 us
    unnamed x5, local copies, waits for them, and re-layouts  2.29 us

profile of v2, /device:TPU:1, one launch (start us, length us, event | category | flops | bytes accessed | tf_op | source)
XLA Modules:
  0.0 70.2 jit_solution(12692502548863040749)
XLA Ops:
  0.0 0.7 convert_element_type.10
  0.7 0.1 reshape.12
  0.8 0.9 %convolution_convert_fusion = s32[32,2,64]{2,0,1:T(8,128)S(1)} fusion(f32[8,64,1]{1,0,2:T(8,128)S(1)} %reshape.12, s32[32,2]{0,1:T(2,128)} %param.9), kind=kOutput, calls=%fused_computation | convolution fusion | flops 397824 | bytes 18688 | tf_op jit(solution)/shard_map/psn,nr->psr/dot_general | solution.py:343
  1.7 0.1 reshape_squeeze.4
  1.8 0.1 pad_add_fusion
  1.9 0.1 reshape.11.ids_ref
  2.0 0.0 copy-start
  2.0 0.9 %copy-done = bf16[1,512,128]{2,1,0:T(8,128)(2,1)S(1)} copy-done((bf16[1,512,128]{2,1,0:T(8,128)(2,1)S(1)}, bf16[1,512,128]{2,1,0:T(8,128)(2,1)}, u32[]{:S(2)}) %copy-start) | copy-done | bytes 131096
  2.9 0.0 copy-start.1
  2.9 0.7 copy-done.1
  3.5 66.0 %stack_adjoint.1 = f32[512,128]{1,0:T(8,128)S(1)} custom-call(s32[2,8]{1,0:T(2,128)S(1)} %copy-done.1, s32[16,384]{1,0:T(8,128)S(1)} %reshape.11.ids_ref, bf16[512,128]{1,0:T(8,128)(2,1)S(1)} %bitcast.8, bf16[2,64,64,128]{3,2,1,0:T(8,128)(2,1)} %obs_hbm.1, f32[16,48,128]{2,1,0:T(8,128)} %constant.4.clone.tab_hbm, bf16[256,1792]{1,0:T(8,128)(2,1)} %constant.5.clone.band_hbm), custom_call_target="tpu_custom_call" | custom-call | tf_op jit(solution)/shard_map/stack_adjoint/pallas_call | solution.py:351
  69.5 0.7 %copy.9 = f32[1,512,128]{2,1,0:T(8,128)} copy(f32[1,512,128]{2,1,0:T(8,128)S(1)} %bitcast.7) | data formatting | bytes 524288
  (2 shorter events, 0.0 us)
Async XLA Ops:
  2.0 0.9 %copy-start = (bf16[1,512,128]{2,1,0:T(8,128)(2,1)S(1)}, bf16[1,512,128]{2,1,0:T(8,128)(2,1)}, u32[]{:S(2)}) copy-start(bf16[1,512,128]{2,1,0:T(8,128)(2,1)} %param.7) | copy-start | bytes 393220
  2.9 0.7 copy-start.1

commit v3 on v2

--- a/solution.py
+++ b/solution.py
@@ -53,8 +53,9 @@
 
 
 def kernel(
-    mask_ref, ids_ref, spec_ref, obs_hbm, tab_hbm, band_hbm, out_ref,
-    stage, xin, amod, bmod, acc, acc_in, obsr, obst, obsf, envo, xst, idc, tab, band,
+    mask_hbm, pb_hbm, memb_hbm, spec_hbm, obs_hbm, tab_hbm, band_hbm, out_ref,
+    mask_ref, pb, memb, spec, sperm, side, ids,
+    stage, xin, amod, bmod, acc, acc_in, obsr, obst, obsf, envo, xst, tab, band,
     rfull, rturn, tbuf, ubuf, outb, rin,
     send_a, recv_a, send_d, recv_d, send_x, recv_x, load,
 ):
@@ -72,9 +73,13 @@
 
     row_a = lax.rem(y_me, 2) * 32 + k_me * 16
     loads = [
-        pltpu.make_async_copy(obs_hbm.at[pp, pl.ds(row_a, 16)], obsr, load.at[0]),
-        pltpu.make_async_copy(band_hbm, band, load.at[1]),
-        pltpu.make_async_copy(tab_hbm, tab, load.at[2]),
+        pltpu.make_async_copy(memb_hbm, memb, load.at[0]),
+        pltpu.make_async_copy(pb_hbm, pb, load.at[1]),
+        pltpu.make_async_copy(spec_hbm.at[0], spec, load.at[2]),
+        pltpu.make_async_copy(mask_hbm, mask_ref, load.at[3]),
+        pltpu.make_async_copy(obs_hbm.at[pp, pl.ds(row_a, 16)], obsr, load.at[4]),
+        pltpu.make_async_copy(band_hbm, band, load.at[5]),
+        pltpu.make_async_copy(tab_hbm, tab, load.at[6]),
     ]
     for copy in loads:
         copy.start()
@@ -91,18 +96,42 @@
     lax.fori_loop(0, NC, greet, 0)
     pl.semaphore_signal(barrier, inc=1, device_id=partner, device_id_type=MESH)
 
-    idc[...] = ids_ref[...].astype(F32).T
-    lane_q = lax.broadcasted_iota(jnp.int32, (NY * ROWS, NQ), 1)
-    lane_s = lax.broadcasted_iota(jnp.int32, (NY * ROWS, NSTA), 1).astype(F32)
-
-    def fill(q, carry):
-        row_id = jnp.sum(jnp.where(lane_q == q, idc[...], 0.0), axis=1, keepdims=True)
-        select = (lane_s == row_id).astype(F32).astype(BF16)
-        rows = dot(select, spec_ref[...]).astype(BF16)
-        stage[pl.ds(q * NY, NY)] = rows.reshape(NY, ROWS, 128)
-        return carry
-
-    lax.fori_loop(0, NQ, fill, 0)
+    lane = lax.broadcasted_iota(jnp.int32, (1, 128), 1)
+    loads[0].wait()
+    column = jnp.concatenate([memb[...], memb[...]], axis=0).astype(F32).T
+    loads[1].wait()
+    pair_col = jnp.concatenate([pb[...]] * 4, axis=0).astype(F32).T
+    loads[2].wait()
+    lane_s = lax.broadcasted_iota(jnp.int32, (128, NSTA), 1).astype(F32)
+    for j in range(4):
+        select = (lane_s == column[:, j : j + 1]).astype(F32).astype(BF16)
+        sperm[j * 128 : (j + 1) * 128, :] = dot(select, spec[...])
+
+    side[0] = jnp.broadcast_to(pair_col[:, 0:1], (32, 128))
+    side[1] = jnp.broadcast_to(pair_col[:, 1:2], (32, 128))
+    both = jnp.where(lane < 64, side[0], side[1])
+    names = jnp.zeros((32, 128), F32)
+    for n in range(NBLK):
+        row = memb[n // 2 : n // 2 + 1, :].astype(F32)
+        other = pltpu.roll(row, 64, 1)
+        row = jnp.where(lane < 64, row, other) if n % 2 == 0 else jnp.where(lane < 64, other, row)
+        names = jnp.where(both == n, row, names)
+    ids[...] = names
+
+    def fill(pair, carry):
+        rows = []
+        for t in range(2):
+            block = side[t, pl.ds(pair, 1), :]
+            picked = sperm[0:64, :]
+            for n in range(1, NBLK):
+                picked = jnp.where(block == n, sperm[n * 64 : (n + 1) * 64, :], picked)
+            rows.append(picked.astype(BF16))
+        for h in range(2):
+            stage[2 * pair + h, 0:32, :] = rows[0][h * 32 : (h + 1) * 32]
+            stage[2 * pair + h, 32:96, :] = rows[1]
+        return carry
+
+    lax.fori_loop(0, 32, fill, 0)
     pl.semaphore_wait(barrier, NC)
 
     def offsets(step):
@@ -152,11 +181,10 @@
     lax.fori_loop(0, NQ, send_all, 0)
     xin[c_me] = stage[c_me]
 
+    loads[3].wait()
     count = jnp.zeros((1, 128), F32)
     for d in range(8):
         count = count + mask_ref[pp, d].astype(F32)
-
-    lane = lax.broadcasted_iota(jnp.int32, (1, 128), 1)
 
     def hilbert(value):
         for j in range(4):
@@ -168,7 +196,7 @@
             [jnp.where(lane < 64, wrapped[j], wrapped[j + 1]) for j in range(4)], axis=1
         )
 
-    loads[0].wait()
+    loads[4].wait()
 
     def turn(a, carry):
         one = obsr[a].astype(F32)
@@ -187,13 +215,13 @@
         return carry
 
     lax.fori_loop(0, N1, place_lags, 0)
-    loads[1].wait()
+    loads[5].wait()
     obs_f = obsf[...]
     hil_o = hilbert(obs_f)
     envo[...] = jnp.sqrt(obs_f * obs_f + hil_o * hil_o)
 
     acc[...] = jnp.zeros_like(acc)
-    loads[2].wait()
+    loads[6].wait()
 
     def forward(step, carry):
         q = source(step)
@@ -291,8 +319,6 @@
                 straight = straight + u * tab[q, CB + n : CB + n + 1, :]
                 crossed = crossed + u * tab[q, SB + n : SB + n + 1, :]
             outb[c, 32:96, :] = (straight + pltpu.roll(crossed, 64, 1)).astype(BF16)
-        for y in range(NY):
-            c = q * NY + y
 
             @pl.when(c != c_me)
             def _():
@@ -307,7 +333,8 @@
     lax.fori_loop(0, NQ, adjoint, 0)
 
     out_ref[...] = jnp.zeros_like(out_ref)
-    station = lax.broadcasted_iota(jnp.int32, (NSTA, NY * ROWS), 0)
+    station = lax.broadcasted_iota(jnp.int32, (NSTA, 128), 0).astype(F32)
+    blank = jnp.zeros((64, 128), BF16)
 
     def gather(step, carry):
         q = source(step)
@@ -318,8 +345,14 @@
             def _():
                 copy_d(c, c).wait_recv()
 
-        place = (station == ids_ref[pl.ds(q, 1), :]).astype(F32).astype(BF16)
-        out_ref[...] += dot(place, rin[pl.ds(q * NY, NY)].reshape(NY * ROWS, 128))
+        for half in range(2):
+            c = q * NY + 2 * half
+            place = (station == ids[pl.ds(2 * q + half, 1), :]).astype(F32).astype(BF16)
+            rows = jnp.concatenate(
+                [rin[c, 0:32, :], rin[c + 1, 0:32, :], rin[c, 32:96, :], blank, rin[c + 1, 32:96, :]],
+                axis=0,
+            )
+            out_ref[...] += dot(jnp.concatenate([place, place], axis=1), rows)
         return carry
 
     lax.fori_loop(0, NQ, gather, 0)
@@ -338,22 +371,21 @@
 
 
 def body(spectra, observed, pair_blocks, members, day_mask):
-    blocks = members.reshape(NBLK, B).astype(F32)
-    pick = (pair_blocks[:, :, None] == jnp.arange(NBLK)[None, None, :]).astype(F32)
-    ids = jnp.einsum("psn,nr->psr", pick, blocks, precision=lax.Precision.HIGHEST)
-    ids = ids.astype(jnp.int32)
-    ids_a = ids[:, 0].reshape(NQ, NY, 32)
-    ids_b = jnp.broadcast_to(ids[:, 1].reshape(NQ, 2, 1, B), (NQ, 2, 2, B)).reshape(NQ, NY, B)
-    ids_all = jnp.concatenate([ids_a, ids_b], axis=2).reshape(NQ, NY * ROWS)
     vm = pl.BlockSpec(memory_space=pltpu.VMEM)
-    sm = pl.BlockSpec(memory_space=pltpu.SMEM)
     hbm = pl.BlockSpec(memory_space=pltpu.HBM)
     return pl.pallas_call(
         kernel,
         out_shape=jax.ShapeDtypeStruct((NSTA, 128), F32),
-        in_specs=[sm, vm, vm, hbm, hbm, hbm],
+        in_specs=[hbm] * 7,
         out_specs=vm,
         scratch_shapes=[
+            pltpu.SMEM((2, 8), jnp.int32),
+            pltpu.VMEM((2, 32), jnp.int32),
+            pltpu.VMEM((4, 128), jnp.int32),
+            pltpu.VMEM((NSTA, 128), BF16),
+            pltpu.VMEM((NSTA, 128), F32),
+            pltpu.VMEM((2, 32, 128), F32),
+            pltpu.VMEM((32, 128), F32),
             pltpu.VMEM((NC, ROWS, 128), BF16),
             pltpu.VMEM((NC, ROWS, 128), BF16),
             pltpu.VMEM((NQ, 512, 512), BF16),
@@ -365,7 +397,6 @@
             pltpu.VMEM((256, 512), F32),
             pltpu.VMEM((256, 512), F32),
             pltpu.VMEM((4 * 256, 128), BF16),
-            pltpu.VMEM((NY * ROWS, NQ), F32),
             pltpu.VMEM((NQ, 2 * (N1 + N2), 128), F32),
             pltpu.VMEM((256, 7 * 256), BF16),
             pltpu.VMEM((2, 256, 512), BF16),
@@ -380,19 +411,25 @@
             pltpu.SemaphoreType.DMA((NC,)),
             pltpu.SemaphoreType.DMA((2,)),
             pltpu.SemaphoreType.DMA((2,)),
-            pltpu.SemaphoreType.DMA((3,)),
+            pltpu.SemaphoreType.DMA((7,)),
         ],
         compiler_params=pltpu.CompilerParams(
             collective_id=0, has_side_effects=True, vmem_limit_bytes=56000000
         ),
         name="stack_adjoint",
     )(
-        day_mask,
-        ids_all,
-        spectra[0],
-        observed,
-        phase_tables(),
-        hilbert_band(),
+        *[
+            pltpu.with_memory_space_constraint(value, pltpu.HBM)
+            for value in (
+                day_mask,
+                pair_blocks.T,
+                members.reshape(4, 128),
+                spectra,
+                observed,
+                phase_tables(),
+                hilbert_band(),
+            )
+        ],
     )[None]
 
 

time: 70.4 us -> 65.8 us (0.935)
  local copies, waits for them, and re-layouts: 2.55 us -> 0.71 us
  Pallas kernels: 66 us -> 64.9 us
  matrix products: 0.89 us -> 0 us
  other arithmetic: 0.77 us -> 0 us
    unnamed x5 -> x1, local copies, waits for them, and re-layouts: 2.29 us -> 0.71 us
    pallas_call x1, Pallas kernels: 66 us -> 64.9 us  [body(): pl.pallas_call(kernel, out_shape=jax.ShapeDtypeStruct((NSTA, 128), F32),...]
    dot_general x1 -> x0, matrix products: 0.89 us -> none  [body(): jnp.einsum('psn,nr->psr', pick, blocks, precision=lax.Precision.HIGHEST)]
where the time goes in v3:
time: 65.8 us; the launch traced here: 65.6 us
  Pallas kernels  64.9 us (99%)
  local copies, waits for them, and re-layouts  0.71 us (1%)
    pallas_call x1, Pallas kernels, body(): pl.pallas_call(kernel, out_shape=jax.ShapeDtypeStruct((NSTA, 128), F32),...  64.9 us

profile of v3, /device:TPU:1, one launch (start us, length us, event | category | flops | bytes accessed | tf_op | source)
XLA Modules:
  0.0 65.6 jit_solution(12124694909202299746)
XLA Ops:
  0.0 64.9 %stack_adjoint.1 = f32[512,128]{1,0:T(8,128)S(1)} custom-call(s32[2,8]{1,0:T(2,128)} %mask_hbm.1, s32[2,32]{1,0:T(2,128)} %bitcast.5, s32[4,128]{1,0:T(4,128)} %bitcast.4, bf16[1,512,128]{2,1,0:T(8,128)(2,1)} %spec_hbm.1, bf16[2,64,64,128]{3,2,1,0:T(8,128)(2,1)} %obs_hbm.1, f32[16,48,128]{2,1,0:T(8,128)} %constant.4.clone.tab_hbm, ...), custom_call_target="tpu_custom_call" | custom-call | tf_op jit(solution)/shard_map/stack_adjoint/pallas_call | solution.py:376
  64.9 0.7 %copy.9 = f32[1,512,128]{2,1,0:T(8,128)} copy(f32[1,512,128]{2,1,0:T(8,128)S(1)} %bitcast.3) | data formatting | bytes 524288

commit v4 on v3

--- a/solution.py
+++ b/solution.py
@@ -55,8 +55,8 @@
 def kernel(
     mask_hbm, pb_hbm, memb_hbm, spec_hbm, obs_hbm, tab_hbm, band_hbm, out_ref,
     mask_ref, pb, memb, spec, sperm, side, ids,
-    stage, xin, amod, bmod, acc, acc_in, obsr, obst, obsf, envo, xst, tab, band,
-    rfull, rturn, tbuf, ubuf, outb, rin,
+    stage, xin, amod_e, amod_o, bmod_e, bmod_o, acc, acc_out, acc_in, obsr, obst, obsf, envo, xst, tab, band,
+    rfull, rturn, tbuf_e, tbuf_o, ubuf_e, ubuf_o, outb, rin,
     send_a, recv_a, send_d, recv_d, send_x, recv_x, load,
 ):
     q_me = lax.axis_index("pairs")
@@ -109,15 +109,6 @@
 
     side[0] = jnp.broadcast_to(pair_col[:, 0:1], (32, 128))
     side[1] = jnp.broadcast_to(pair_col[:, 1:2], (32, 128))
-    both = jnp.where(lane < 64, side[0], side[1])
-    names = jnp.zeros((32, 128), F32)
-    for n in range(NBLK):
-        row = memb[n // 2 : n // 2 + 1, :].astype(F32)
-        other = pltpu.roll(row, 64, 1)
-        row = jnp.where(lane < 64, row, other) if n % 2 == 0 else jnp.where(lane < 64, other, row)
-        names = jnp.where(both == n, row, names)
-    ids[...] = names
-
     def fill(pair, carry):
         rows = []
         for t in range(2):
@@ -181,10 +172,21 @@
     lax.fori_loop(0, NQ, send_all, 0)
     xin[c_me] = stage[c_me]
 
+    both = jnp.where(lane < 64, side[0], side[1])
+    names = jnp.zeros((32, 128), F32)
+    for n in range(NBLK):
+        row = memb[n // 2 : n // 2 + 1, :].astype(F32)
+        other = pltpu.roll(row, 64, 1)
+        row = jnp.where(lane < 64, row, other) if n % 2 == 0 else jnp.where(lane < 64, other, row)
+        names = jnp.where(both == n, row, names)
+    ids[...] = names
+
+
     loads[3].wait()
     count = jnp.zeros((1, 128), F32)
     for d in range(8):
         count = count + mask_ref[pp, d].astype(F32)
+    share_of = jnp.concatenate([(1.0 / 32.0) / count] * 4, axis=1)
 
     def hilbert(value):
         for j in range(4):
@@ -223,7 +225,9 @@
     acc[...] = jnp.zeros_like(acc)
     loads[6].wait()
 
-    def forward(step, carry):
+    amods, bmods = (amod_e, amod_o), (bmod_e, bmod_o)
+
+    def rotate(step, slot, odd):
         q = source(step)
         for y in range(NY):
             c = q * NY + y
@@ -232,32 +236,61 @@
             def _():
                 copy_a(c, c).wait_recv()
 
+        amod, bmod = amods[odd], bmods[odd]
         for y in range(NY):
-            keep = mask_ref[pp, 2 * y + k_me].astype(F32)
-            x = xin[q * NY + y].astype(F32) * keep
+            x = xin[q * NY + y].astype(F32) * mask_ref[pp, 2 * y + k_me].astype(F32)
             xr = pltpu.roll(x, 64, 1)
             lanes = slice(y * 128, (y + 1) * 128)
             for h in range(2):
                 rows = slice(h * 16, (h + 1) * 16)
                 for n in range(N1):
-                    turned = x[rows] * tab[q, CA + n : CA + n + 1, :] + xr[rows] * tab[q, SA + n : SA + n + 1, :]
-                    amod[q, h * 256 + n * 16 : h * 256 + (n + 1) * 16, lanes] = turned.astype(BF16)
+                    turned = x[rows] * tab[q, CA + n : CA + n + 1, :]
+                    turned = turned + xr[rows] * tab[q, SA + n : SA + n + 1, :]
+                    amod[slot, h * 256 + n * 16 : h * 256 + (n + 1) * 16, lanes] = turned.astype(BF16)
             for n in range(N2):
-                turned = x[32:] * tab[q, CB + n : CB + n + 1, :] + xr[32:] * tab[q, SB + n : SB + n + 1, :]
-                bmod[q, n * 64 : (n + 1) * 64, lanes] = turned.astype(BF16)
-        for h in range(2):
-            acc[h] += lax.dot_general(
-                amod[q, h * 256 : (h + 1) * 256, :],
-                bmod[q],
-                (((1,), (1,)), ((), ())),
-                preferred_element_type=F32,
-            )
-        return carry
-
-    lax.fori_loop(0, NQ, forward, 0)
-
+                turned = x[32:] * tab[q, CB + n : CB + n + 1, :]
+                turned = turned + xr[32:] * tab[q, SB + n : SB + n + 1, :]
+                bmod[slot, n * 64 : (n + 1) * 64, lanes] = turned.astype(BF16)
+
+    def correlate(slot, odd):
+        acc[...] += lax.dot_general(
+            amods[odd][slot],
+            bmods[odd][slot],
+            (((1,), (1,)), ((), ())),
+            preferred_element_type=F32,
+        ).reshape(2, 256, 512)
+
+    rotate(0, 0, 0)
+
+    def forward(i, carry):
+        rotate(2 * i + 1, i, 1)
+        correlate(i, 0)
+        rotate(2 * i + 2, i + 1, 0)
+        correlate(i, 1)
+        return carry
+
+    lax.fori_loop(0, NQ // 2 - 1, forward, 0)
+    correlate(NQ // 2 - 1, 0)
+    rotate(NQ - 1, NQ // 2 - 1, 1)
+    rows_mine = pl.ds(pl.multiple_of(k_me * 256, 256), 256)
+    rows_other = pl.ds(pl.multiple_of((1 - k_me) * 256, 256), 256)
+
+    def last_half(rows):
+        return lax.dot_general(
+            amod_o[NQ // 2 - 1, rows, :],
+            bmod_o[NQ // 2 - 1],
+            (((1,), (1,)), ((), ())),
+            preferred_element_type=F32,
+        )
+
+    def slot_of(step):
+        dx, dz = offsets(step)
+        dx, dz = lax.rem(4 - dx, 4), lax.rem(4 - dz, 4)
+        return (15 - 4 * lax.rem(dz + 6 - dx, 4) - lax.rem(dx + 2, 4)) // 2
+
+    acc_out[...] = (acc[1 - k_me] + last_half(rows_other)).astype(BF16)
     swap = pltpu.make_async_remote_copy(
-        src_ref=acc.at[1 - k_me],
+        src_ref=acc_out,
         dst_ref=acc_in,
         send_sem=send_x.at[0],
         recv_sem=recv_x.at[0],
@@ -265,15 +298,15 @@
         device_id_type=MESH,
     )
     swap.start()
+    acc[k_me] += last_half(rows_mine)
     swap.wait_recv()
-    lanes_count = jnp.concatenate([count] * 4, axis=1)
-    stacked = (acc[k_me] + acc_in[...]) * (1.0 / 32.0) / lanes_count
+    stacked = (acc[k_me] + acc_in[...].astype(F32)) * share_of
     hil_s = hilbert(stacked)
     env_s = jnp.sqrt(stacked * stacked + hil_s * hil_s)
     residual = (stacked - obsf[...]) * (
         (1.0 + env_s) / (1.0 + env_s + envo[...])
     )
-    rfull[k_me] = (residual * (1.0 / 32.0) / lanes_count).astype(BF16)
+    rfull[k_me] = (residual * share_of).astype(BF16)
     share = pltpu.make_async_remote_copy(
         src_ref=rfull.at[k_me],
         dst_ref=rfull.at[k_me],
@@ -283,6 +316,10 @@
         device_id_type=MESH,
     )
     share.start()
+    rturn[k_me] = rfull[k_me].T
+    first = slot_of(0)
+    tbuf_e[rows_mine, :] = dot(rfull[k_me], bmod_e[first])
+    ubuf_e[...] = dot(rturn[k_me], amod_e[first, rows_mine, :])
     pltpu.make_async_remote_copy(
         src_ref=rfull.at[1 - k_me],
         dst_ref=rfull.at[1 - k_me],
@@ -291,15 +328,23 @@
         device_id=partner,
         device_id_type=MESH,
     ).wait_recv()
-    rturn[...] = rfull[...].reshape(512, 512).T
-
-    def adjoint(step, carry):
+    rturn[1 - k_me] = rfull[1 - k_me].T
+    tbuf_e[rows_other, :] = dot(rfull[1 - k_me], bmod_e[first])
+    ubuf_e[...] += dot(rturn[1 - k_me], amod_e[first, rows_other, :])
+
+    tbufs, ubufs = (tbuf_e, tbuf_o), (ubuf_e, ubuf_o)
+
+    def spread_a(step, odd):
+        tbufs[odd][...] = dot(rfull[...].reshape(512, 512), bmods[odd][slot_of(step)])
+
+    def spread_b(step, odd):
+        turned = jnp.concatenate([rturn[0], rturn[1]], axis=1)
+        ubufs[odd][...] = dot(turned, amods[odd][slot_of(step)])
+
+    def unrotate(step, odd, days):
         q = target(step)
-        for h in range(2):
-            tbuf[h * 256 : (h + 1) * 256, :] = dot(rfull[h], bmod[q])
-        for h in range(2):
-            ubuf[h * 256 : (h + 1) * 256, :] = dot(rturn[h * 256 : (h + 1) * 256, :], amod[q])
-        for y in range(NY):
+        tbuf, ubuf = tbufs[odd], ubufs[odd]
+        for y in days:
             c = q * NY + y
             lanes = slice(y * 128, (y + 1) * 128)
             for h in range(2):
@@ -320,17 +365,43 @@
                 crossed = crossed + u * tab[q, SB + n : SB + n + 1, :]
             outb[c, 32:96, :] = (straight + pltpu.roll(crossed, 64, 1)).astype(BF16)
 
+    def post(step):
+        q = target(step)
+        for dy in (2, 1, 3, 0):
+            c = q * NY + lax.rem(y_me + dy, NY)
+
             @pl.when(c != c_me)
             def _():
                 copy_d(c, c_me).start()
 
-            @pl.when(c == c_me)
+    def settle(step, copy_of):
+        q = target(step)
+        for y in range(NY):
+            c = q * NY + y
+
+            @pl.when(c != c_me)
             def _():
-                rin[c_me] = outb[c_me]
-
-        return carry
-
-    lax.fori_loop(0, NQ, adjoint, 0)
+                copy_of(c, c_me).wait_send()
+
+    def both_steps(step, odd):
+        spread_a(step + 1, 1 - odd)
+        unrotate(step, odd, (0, 1))
+        spread_b(step + 1, 1 - odd)
+        unrotate(step, odd, (2, 3))
+        post(step)
+        settle(step, copy_a)
+
+    def adjoint(i, carry):
+        both_steps(2 * i, 0)
+        both_steps(2 * i + 1, 1)
+        return carry
+
+    lax.fori_loop(0, NQ // 2 - 1, adjoint, 0)
+    both_steps(NQ - 2, 0)
+    unrotate(NQ - 1, 1, range(NY))
+    post(NQ - 1)
+    settle(NQ - 1, copy_a)
+    rin[c_me] = outb[c_me]
 
     out_ref[...] = jnp.zeros_like(out_ref)
     station = lax.broadcasted_iota(jnp.int32, (NSTA, 128), 0).astype(F32)
@@ -353,19 +424,11 @@
                 axis=0,
             )
             out_ref[...] += dot(jnp.concatenate([place, place], axis=1), rows)
+        settle(step, copy_d)
         return carry
 
     lax.fori_loop(0, NQ, gather, 0)
 
-    def drain(c, carry):
-        @pl.when(c != c_me)
-        def _():
-            copy_a(c, c_me).wait_send()
-            copy_d(c, c_me).wait_send()
-
-        return carry
-
-    lax.fori_loop(0, NC, drain, 0)
     swap.wait_send()
     share.wait_send()
 
@@ -388,10 +451,13 @@
             pltpu.VMEM((32, 128), F32),
             pltpu.VMEM((NC, ROWS, 128), BF16),
             pltpu.VMEM((NC, ROWS, 128), BF16),
-            pltpu.VMEM((NQ, 512, 512), BF16),
-            pltpu.VMEM((NQ, 512, 512), BF16),
+            pltpu.VMEM((NQ // 2, 512, 512), BF16),
+            pltpu.VMEM((NQ // 2, 512, 512), BF16),
+            pltpu.VMEM((NQ // 2, 512, 512), BF16),
+            pltpu.VMEM((NQ // 2, 512, 512), BF16),
             pltpu.VMEM((2, 256, 512), F32),
-            pltpu.VMEM((256, 512), F32),
+            pltpu.VMEM((256, 512), BF16),
+            pltpu.VMEM((256, 512), BF16),
             pltpu.VMEM((16, B, L), BF16),
             pltpu.VMEM((16 * L, 128), F32),
             pltpu.VMEM((256, 512), F32),
@@ -400,7 +466,9 @@
             pltpu.VMEM((NQ, 2 * (N1 + N2), 128), F32),
             pltpu.VMEM((256, 7 * 256), BF16),
             pltpu.VMEM((2, 256, 512), BF16),
-            pltpu.VMEM((512, 512), BF16),
+            pltpu.VMEM((2, 512, 256), BF16),
+            pltpu.VMEM((512, 512), F32),
+            pltpu.VMEM((512, 512), F32),
             pltpu.VMEM((512, 512), F32),
             pltpu.VMEM((512, 512), F32),
             pltpu.VMEM((NC, ROWS, 128), BF16),

time: 65.8 us -> 64.8 us (0.985)
  Pallas kernels: 64.9 us -> 64 us
    pallas_call x1, Pallas kernels: 64.9 us -> 64 us  [body(): pl.pallas_call(kernel, out_shape=jax.ShapeDtypeStruct((NSTA, 128), F32),...]
where the time goes in v4:
time: 64.8 us; the launch traced here: 64.7 us
  Pallas kernels  64 us (99%)
  local copies, waits for them, and re-layouts  0.71 us (1%)
    pallas_call x1, Pallas kernels, body(): pl.pallas_call(kernel, out_shape=jax.ShapeDtypeStruct((NSTA, 128), F32),...  64 us

profile of v4, /device:TPU:1, one launch (start us, length us, event | category | flops | bytes accessed | tf_op | source)
XLA Modules:
  0.0 64.7 jit_solution(10135775214458382569)
XLA Ops:
  0.0 64.0 %stack_adjoint.1 = f32[512,128]{1,0:T(8,128)S(1)} custom-call(s32[2,8]{1,0:T(2,128)} %mask_hbm.1, s32[2,32]{1,0:T(2,128)} %bitcast.5, s32[4,128]{1,0:T(4,128)} %bitcast.4, bf16[1,512,128]{2,1,0:T(8,128)(2,1)} %spec_hbm.1, bf16[2,64,64,128]{3,2,1,0:T(8,128)(2,1)} %obs_hbm.1, f32[16,48,128]{2,1,0:T(8,128)} %constant.4.clone.tab_hbm, ...), custom_call_target="tpu_custom_call" | custom-call | tf_op jit(solution)/shard_map/stack_adjoint/pallas_call | solution.py:439
  64.0 0.7 %copy.9 = f32[1,512,128]{2,1,0:T(8,128)} copy(f32[1,512,128]{2,1,0:T(8,128)S(1)} %bitcast.3) | data formatting | bytes 524288

commit v5 on v4

--- a/solution.py
+++ b/solution.py
@@ -459,7 +459,7 @@
             pltpu.VMEM((256, 512), BF16),
             pltpu.VMEM((256, 512), BF16),
             pltpu.VMEM((16, B, L), BF16),
-            pltpu.VMEM((16 * L, 128), F32),
+            pltpu.VMEM((17 * L, 128), F32),
             pltpu.VMEM((256, 512), F32),
             pltpu.VMEM((256, 512), F32),
             pltpu.VMEM((4 * 256, 128), BF16),

time: 64.8 us -> 64.8 us (level)
  no operation moved by 1% of the time
where the time goes in v5:
time: 64.8 us; the launch traced here: 64.7 us
  Pallas kernels  64 us (99%)
  local copies, waits for them, and re-layouts  0.71 us (1%)
    pallas_call x1, Pallas kernels, body(): pl.pallas_call(kernel, out_shape=jax.ShapeDtypeStruct((NSTA, 128), F32),...  64 us

profile of v5, /device:TPU:1, one launch (start us, length us, event | category | flops | bytes accessed | tf_op | source)
XLA Modules:
  0.0 64.7 jit_solution(5617915280839055999)
XLA Ops:
  0.0 64.0 %stack_adjoint.1 = f32[512,128]{1,0:T(8,128)S(1)} custom-call(s32[2,8]{1,0:T(2,128)} %mask_hbm.1, s32[2,32]{1,0:T(2,128)} %bitcast.5, s32[4,128]{1,0:T(4,128)} %bitcast.4, bf16[1,512,128]{2,1,0:T(8,128)(2,1)} %spec_hbm.1, bf16[2,64,64,128]{3,2,1,0:T(8,128)(2,1)} %obs_hbm.1, f32[16,48,128]{2,1,0:T(8,128)} %constant.4.clone.tab_hbm, ...), custom_call_target="tpu_custom_call" | custom-call | tf_op jit(solution)/shard_map/stack_adjoint/pallas_call | solution.py:439
  64.0 0.7 %copy.9 = f32[1,512,128]{2,1,0:T(8,128)} copy(f32[1,512,128]{2,1,0:T(8,128)S(1)} %bitcast.3) | data formatting | bytes 524288
